TPU v7x, 32 devices: a whole 2x2x4 slice. The times are simulated.
32 devices in a mesh: outer: 8 (over y, x, core), inner: 4 (over z).
Axes of the slice: x: 2, y: 2, z: 4, core: 2. Of those that a mesh axis runs over, the one named last changes fastest.
Arguments:
- query_image: bfloat16 [2048, 1024], P(('outer', 'inner')), may hold values from -6 to 6
- key_image: bfloat16 [2048, 1024], P(('outer', 'inner')), may hold values from -6 to 6
- value_image: bfloat16 [2048, 1024], P(('outer', 'inner')), may hold values from -6 to 6
- attended_image: bfloat16 [2048, 1024], P(('outer', 'inner')), may hold values from -6 to 6
- upstream_image: bfloat16 [2048, 1024], P(('outer', 'inner')), may hold values from -128 to 128
- logsum_image: float32 [2048, 8], P(('outer', 'inner')), may hold values from 8.6 to 9.4
- query_text: bfloat16 [512, 1024], P(None, 'outer'), may hold values from -6 to 6
- key_text: bfloat16 [512, 1024], P(None, 'outer'), may hold values from -6 to 6
- value_text: bfloat16 [512, 1024], P(None, 'outer'), may hold values from -6 to 6
- attended_text: bfloat16 [512, 1024], P(None, 'outer'), may hold values from -6 to 6
- upstream_text: bfloat16 [512, 1024], P(None, 'outer'), may hold values from -128 to 128
- logsum_text: float32 [512, 8], P(None, 'outer'), may hold values from 8.6 to 9.4
Outputs:
- grad_query_image: bfloat16 [2048, 1024], P(('outer', 'inner'))
- grad_key_image: bfloat16 [2048, 1024], P(('outer', 'inner'))
- grad_value_image: bfloat16 [2048, 1024], P(('outer', 'inner'))
- grad_query_text: bfloat16 [512, 1024], P('inner', 'outer')
- grad_key_text: bfloat16 [512, 1024], P('inner', 'outer')
- grad_value_text: bfloat16 [512, 1024], P('inner', 'outer')
All inputs are finite; a program needn't handle non-finite values.
Results may differ from a plain program's by a relative error of at most 0.0055.
Values may be sent and summed in bfloat16 or wider, within the bound.
A program may use at most 64 MiB of HBM per device.

v0:
```python
import math

import jax
import jax.numpy as jnp
from jax import lax
from jax.sharding import PartitionSpec as P

HEAD_DIM = 128


def across_rows(left, right):
    return lax.dot_general(
        left, right, (((1,), (1,)), ((), ())), preferred_element_type=jnp.float32
    )


def down_rows(left, right):
    return lax.dot_general(
        left, right, (((0,), (0,)), ((), ())), preferred_element_type=jnp.float32
    )


def weights_and_mixed(queries, upstream, log_sums, deltas, keys, values):
    scores = across_rows(queries, keys) * HEAD_DIM ** (-0.5)
    weights = jnp.exp(scores - log_sums)
    slopes = across_rows(upstream, values)
    mixed = weights * (slopes - deltas)
    return (weights.astype(jnp.bfloat16), mixed.astype(jnp.bfloat16))


def query_side(mixed_half, keys):
    return jnp.dot(mixed_half, keys, preferred_element_type=jnp.float32) * HEAD_DIM ** (-0.5)


def key_side(weights_half, mixed_half, queries, upstream):
    grad_values = down_rows(weights_half, upstream)
    grad_keys = down_rows(mixed_half, queries) * HEAD_DIM ** (-0.5)
    return (grad_keys, grad_values)


def shards(
    query_image,
    key_image,
    value_image,
    attended_image,
    upstream_image,
    logsum_image,
    query_text,
    key_text,
    value_text,
    attended_text,
    upstream_text,
    logsum_text,
):
    queries, keys, values, upstream, attended = (
        lax.all_to_all(query_image, "outer", split_axis=1, concat_axis=0, tiled=True),
        lax.all_to_all(key_image, "outer", split_axis=1, concat_axis=0, tiled=True),
        lax.all_to_all(value_image, "outer", split_axis=1, concat_axis=0, tiled=True),
        lax.all_to_all(upstream_image, "outer", split_axis=1, concat_axis=0, tiled=True),
        lax.all_to_all(attended_image, "outer", split_axis=1, concat_axis=0, tiled=True),
    )
    log_sums = lax.all_to_all(logsum_image, "outer", split_axis=1, concat_axis=0, tiled=True)
    deltas = jnp.sum(
        upstream.astype(jnp.float32) * attended.astype(jnp.float32), axis=1, keepdims=True
    )
    text_deltas = jnp.sum(
        upstream_text.astype(jnp.float32) * attended_text.astype(jnp.float32), axis=1, keepdims=True
    )
    weights_half, mixed_half = weights_and_mixed(
        queries, upstream, log_sums, deltas, key_text, value_text
    )
    grad_query_near = query_side(mixed_half, key_text)
    text_key_first, text_value_first = key_side(weights_half, mixed_half, queries, upstream)
    weights_half, mixed_half = weights_and_mixed(
        query_text, upstream_text, logsum_text, text_deltas, keys, values
    )
    text_query_first = query_side(mixed_half, keys)
    grad_key_near, grad_value_near = key_side(weights_half, mixed_half, query_text, upstream_text)
    share = query_text.shape[0] // lax.axis_size("inner")
    first_row = lax.axis_index("inner") * share

    def text_rows(matrix):
        return lax.dynamic_slice_in_dim(matrix, first_row, share, 0)

    own_queries = text_rows(query_text)
    own_upstream = text_rows(upstream_text)
    weights_half, mixed_half = weights_and_mixed(
        own_queries,
        own_upstream,
        text_rows(logsum_text),
        text_rows(text_deltas),
        key_text,
        value_text,
    )
    text_query_rows = query_side(mixed_half, key_text)
    text_key_second, text_value_second = key_side(
        weights_half, mixed_half, own_queries, own_upstream
    )
    text_query = lax.dynamic_update_slice_in_dim(
        text_query_first, text_rows(text_query_first) + text_query_rows, first_row, 0
    )
    zero_rows = jnp.zeros(queries.shape, jnp.float32)
    whole_keys, whole_values = (
        lax.all_gather(keys, "inner", axis=0, tiled=True),
        lax.all_gather(values, "inner", axis=0, tiled=True),
    )
    key_count = whole_keys.shape[0]
    size = math.gcd(key_count, 1024)
    count = key_count // size
    stacked_keys = whole_keys.reshape(count, size, whole_keys.shape[1])
    stacked_values = whole_values.reshape(count, size, whole_values.shape[1])

    def key_block(carry, block):
        weights_block, mixed_block = weights_and_mixed(
            queries, upstream, log_sums, deltas, block[0], block[1]
        )
        terms = key_side(weights_block, mixed_block, queries, upstream)
        return (carry + query_side(mixed_block, block[0]), terms)

    grad_query_far, stacked_terms = lax.scan(key_block, zero_rows, (stacked_keys, stacked_values))
    key_terms = stacked_terms[0].reshape(key_count, whole_keys.shape[1])
    value_terms = stacked_terms[1].reshape(key_count, whole_keys.shape[1])
    grad_key_far, grad_value_far = (
        lax.psum_scatter(key_terms, "inner", scatter_dimension=0, tiled=True),
        lax.psum_scatter(value_terms, "inner", scatter_dimension=0, tiled=True),
    )
    head_grads = (
        (grad_query_near + grad_query_far).astype(jnp.bfloat16),
        (grad_key_near + grad_key_far).astype(jnp.bfloat16),
        (grad_value_near + grad_value_far).astype(jnp.bfloat16),
    )
    image_query, image_key, image_value = (
        lax.all_to_all(head_grads[0], "outer", split_axis=0, concat_axis=1, tiled=True),
        lax.all_to_all(head_grads[1], "outer", split_axis=0, concat_axis=1, tiled=True),
        lax.all_to_all(head_grads[2], "outer", split_axis=0, concat_axis=1, tiled=True),
    )
    summed_query, summed_key, summed_value = (
        lax.psum_scatter(text_query, "inner", scatter_dimension=0, tiled=True),
        lax.psum_scatter(
            text_key_first + text_key_second, "inner", scatter_dimension=0, tiled=True
        ),
        lax.psum_scatter(
            text_value_first + text_value_second, "inner", scatter_dimension=0, tiled=True
        ),
    )
    return (
        image_query,
        image_key,
        image_value,
        summed_query.astype(jnp.bfloat16),
        summed_key.astype(jnp.bfloat16),
        summed_value.astype(jnp.bfloat16),
    )


def solution(mesh):
    in_specs = (
        P(("outer", "inner"), None),
        P(("outer", "inner"), None),
        P(("outer", "inner"), None),
        P(("outer", "inner"), None),
        P(("outer", "inner"), None),
        P(("outer", "inner"), None),
        P(None, "outer"),
        P(None, "outer"),
        P(None, "outer"),
        P(None, "outer"),
        P(None, "outer"),
        P(None, "outer"),
    )
    out_specs = (
        P(("outer", "inner"), None),
        P(("outer", "inner"), None),
        P(("outer", "inner"), None),
        P("inner", "outer"),
        P("inner", "outer"),
        P("inner", "outer"),
    )
    return jax.shard_map(shards, mesh=mesh, in_specs=in_specs, out_specs=out_specs, check_vma=False)
```

profile of v0, /device:TPU:0, one launch (start us, length us, event | category | flops | bytes accessed | tf_op | source)
XLA Modules:
  0.0 203.6 jit_solution(8097618321480912621)
XLA Ops:
  7.2 5.3 %all-to-all-start.1 = ((f32[64,8,1]{0,2,1:T(1,128)}), f32[64,8,1]{0,2,1:T(1,128)S(1)}, u32[]{:S(2)}, u32[]{:S(2)}) async-start(f32[64,8,1]{0,2,1:T(1,128)} %bitcast.168), calls=%async_computation.1 | async-start | bytes 8192 | tf_op jit(solution)/shard_map/all_to_all | solution.py:62
  22.0 4.2 %all-to-all-start.4 = ((bf16[64,8,128]{2,0,1:T(8,128)(2,1)}), bf16[64,8,128]{2,0,1:T(8,128)(2,1)S(1)}, u32[]{:S(2)}, u32[]{:S(2)}) async-start(bf16[64,8,128]{2,0,1:T(8,128)(2,1)} %copy_bitcast_fusion.4), calls=%async_computation.4 | async-start | bytes 262144 | tf_op jit(solution)/shard_map/all_to_all | solution.py:57
  27.1 4.6 %all-to-all-done.4 = bf16[64,8,128]{2,0,1:T(8,128)(2,1)S(1)} async-done(((bf16[64,8,128]{2,0,1:T(8,128)(2,1)}), bf16[64,8,128]{2,0,1:T(8,128)(2,1)S(1)}, u32[]{:S(2)}, u32[]{:S(2)}) %all-to-all-start.4) | async-done | bytes 131104 | tf_op jit(solution)/shard_map/all_to_all | solution.py:57
  31.7 3.4 %all-to-all-start.5 = ((bf16[64,8,128]{2,0,1:T(8,128)(2,1)}), bf16[64,8,128]{2,0,1:T(8,128)(2,1)S(1)}, u32[]{:S(2)}, u32[]{:S(2)}) async-start(bf16[64,8,128]{2,0,1:T(8,128)(2,1)} %copy_bitcast_fusion.3), calls=%async_computation.5 | async-start | bytes 262144 | tf_op jit(solution)/shard_map/all_to_all | solution.py:58
  35.4 5.1 %all-to-all-done.5 = bf16[64,8,128]{2,0,1:T(8,128)(2,1)S(1)} async-done(((bf16[64,8,128]{2,0,1:T(8,128)(2,1)}), bf16[64,8,128]{2,0,1:T(8,128)(2,1)S(1)}, u32[]{:S(2)}, u32[]{:S(2)}) %all-to-all-start.5) | async-done | bytes 131104 | tf_op jit(solution)/shard_map/all_to_all | solution.py:58
  40.5 3.4 %all-to-all-start.2 = ((bf16[64,8,128]{2,0,1:T(8,128)(2,1)}), bf16[64,8,128]{2,0,1:T(8,128)(2,1)S(1)}, u32[]{:S(2)}, u32[]{:S(2)}) async-start(bf16[64,8,128]{2,0,1:T(8,128)(2,1)} %copy_bitcast_fusion.6), calls=%async_computation.2 | async-start | bytes 262144 | tf_op jit(solution)/shard_map/all_to_all | solution.py:59
  45.3 4.0 %all-to-all-done.2 = bf16[64,8,128]{2,0,1:T(8,128)(2,1)S(1)} async-done(((bf16[64,8,128]{2,0,1:T(8,128)(2,1)}), bf16[64,8,128]{2,0,1:T(8,128)(2,1)S(1)}, u32[]{:S(2)}, u32[]{:S(2)}) %all-to-all-start.2) | async-done | bytes 131104 | tf_op jit(solution)/shard_map/all_to_all | solution.py:59
  49.3 3.4 %all-to-all-start.3 = ((bf16[64,8,128]{2,0,1:T(8,128)(2,1)}), bf16[64,8,128]{2,0,1:T(8,128)(2,1)S(1)}, u32[]{:S(2)}, u32[]{:S(2)}) async-start(bf16[64,8,128]{2,0,1:T(8,128)(2,1)} %copy_bitcast_fusion.5), calls=%async_computation.3 | async-start | bytes 262144 | tf_op jit(solution)/shard_map/all_to_all | solution.py:60
  52.9 5.2 %all-to-all-done.3 = bf16[64,8,128]{2,0,1:T(8,128)(2,1)S(1)} async-done(((bf16[64,8,128]{2,0,1:T(8,128)(2,1)}), bf16[64,8,128]{2,0,1:T(8,128)(2,1)S(1)}, u32[]{:S(2)}, u32[]{:S(2)}) %all-to-all-start.3) | async-done | bytes 131104 | tf_op jit(solution)/shard_map/all_to_all | solution.py:60
  58.1 3.4 %all-to-all-start = ((bf16[64,8,128]{2,0,1:T(8,128)(2,1)}), bf16[64,8,128]{2,0,1:T(8,128)(2,1)S(1)}, u32[]{:S(2)}, u32[]{:S(2)}) async-start(bf16[64,8,128]{2,0,1:T(8,128)(2,1)} %copy_bitcast_fusion.7), calls=%async_computation | async-start | bytes 262144 | tf_op jit(solution)/shard_map/all_to_all | solution.py:56
  62.3 4.6 %all-to-all-done = bf16[64,8,128]{2,0,1:T(8,128)(2,1)S(1)} async-done(((bf16[64,8,128]{2,0,1:T(8,128)(2,1)}), bf16[64,8,128]{2,0,1:T(8,128)(2,1)S(1)}, u32[]{:S(2)}, u32[]{:S(2)}) %all-to-all-start) | async-done | bytes 131104 | tf_op jit(solution)/shard_map/all_to_all | solution.py:56
  67.6 19.9 %all_gather.6 = bf16[2048,128]{1,0:T(8,128)(2,1)S(1)} all-gather(bf16[512,128]{1,0:T(8,128)(2,1)S(1)} %bitcast.158), channel_id=1, replica_groups=mesh['outer'=8,'inner'=4] {'inner'}, dimensions={0}, use_global_device_ids=true | all-gather | bytes 655360 | tf_op jit(solution)/shard_map/all_gather | solution.py:104
  88.9 17.1 %all_gather.7 = bf16[2048,128]{1,0:T(8,128)(2,1)} all-gather(bf16[512,128]{1,0:T(8,128)(2,1)S(1)} %bitcast.160), channel_id=1, replica_groups=mesh['outer'=8,'inner'=4] {'inner'}, dimensions={0}, use_global_device_ids=true | all-gather | bytes 655360 | tf_op jit(solution)/shard_map/all_gather | solution.py:105
  107.4 13.6 %while.15 = (s32[]{:T(128)}, f32[512,128]{1,0:T(8,128)}, f32[2,1024,128]{2,1,0:T(8,128)}, f32[2,1024,128]{2,1,0:T(8,128)}, bf16[2,1024,128]{2,1,0:T(8,128)(2,1)S...) while((s32[]{:T(128)}, f32[512,128]{1,0:T(8,128)}, ...), condition=%wide.region_2.3_spmd.clone, body=%wide.region_1.0_spmd.clone.sunk | while | flops 675610624 | bytes 27007272 | solution.py:120
  109.2 2.2 %fusion.116 = f32[512,128]{1,0:T(8,128)} fusion(bf16[1024,512]{1,0:T(8,128)(2,1)S(1)} %multiply_convert_fusion.2, f32[512,128]{1,0:T(8,128)} %get-tuple-element.190, bf16[2,1024,128]{2,1,0:T(8,128)(2,1)} %copy-done.1, s32[]{:T(128)S(6)} %copy.62, pred[]{:T(512)S(6)} %compare.3), kind=kOutput, calls=%fused_computation.9.clone.1 | convolution fusion | flops 134414336 | bytes 1835013 | tf_op jit(solution)/shard_map/while/body/eval_jaxpr/dot_general | solution.py:32
  116.0 2.3 %fusion.116 = f32[512,128]{1,0:T(8,128)} fusion(bf16[1024,512]{1,0:T(8,128)(2,1)S(1)} %multiply_convert_fusion.2, f32[512,128]{1,0:T(8,128)} %get-tuple-element.190, bf16[2,1024,128]{2,1,0:T(8,128)(2,1)} %copy-done.1, s32[]{:T(128)S(6)} %copy.62, pred[]{:T(512)S(6)} %compare.3), kind=kOutput, calls=%fused_computation.9.clone.1 | convolution fusion | flops 134414336 | bytes 1835013 | tf_op jit(solution)/shard_map/while/body/eval_jaxpr/dot_general | solution.py:32
  122.4 7.9 %all_to_all.165 = bf16[8,64,128]{2,1,0:T(8,128)(2,1)S(1)} all-to-all(bf16[8,64,128]{2,1,0:T(8,128)(2,1)S(1)} %bitcast.163), channel_id=1, replica_groups=mesh['outer'=8,'inner'=4] {'outer'}, dimensions={0} | all-to-all | bytes 262144 | tf_op jit(solution)/shard_map/all_to_all | solution.py:133
  135.3 22.0 %reduce-scatter.6.cloned.1.call-done = f32[512,128]{1,0:T(8,128)} async-done(((f32[2048,128]{1,0:T(8,128)}), f32[512,128]{1,0:T(8,128)}) %reduce-scatter.6.cloned.1.call-update) | async-done | bytes 262160 | tf_op jit(solution)/shard_map/reduce_scatter | solution.py:124
  157.3 2.0 fusion.35
  159.3 3.6 %all-to-all-start.7 = ((bf16[8,64,128]{2,1,0:T(8,128)(2,1)}), bf16[8,64,128]{2,1,0:T(8,128)(2,1)S(1)}, u32[]{:S(2)}, u32[]{:S(2)}) async-start(bf16[8,64,128]{2,1,0:T(8,128)(2,1)} %bitcast.21), calls=%async_computation.8 | async-start | bytes 262144 | tf_op jit(solution)/shard_map/all_to_all | solution.py:134
  162.9 22.3 %reduce-scatter.8.cloned.1.call-done = f32[512,128]{1,0:T(8,128)} async-done(((f32[2048,128]{1,0:T(8,128)}), f32[512,128]{1,0:T(8,128)}) %reduce-scatter.8.cloned.1.call-update) | async-done | bytes 262160 | tf_op jit(solution)/shard_map/reduce_scatter | solution.py:125
  185.3 2.0 fusion.33
  187.2 3.6 %all-to-all-start.8 = ((bf16[8,64,128]{2,1,0:T(8,128)(2,1)}), bf16[8,64,128]{2,1,0:T(8,128)(2,1)S(1)}, u32[]{:S(2)}, u32[]{:S(2)}) async-start(bf16[8,64,128]{2,1,0:T(8,128)(2,1)} %bitcast.24), calls=%async_computation.10 | async-start | bytes 262144 | tf_op jit(solution)/shard_map/all_to_all | solution.py:135
  191.5 4.8 %all-to-all-done.8 = bf16[8,64,128]{2,1,0:T(8,128)(2,1)S(1)} async-done(((bf16[8,64,128]{2,1,0:T(8,128)(2,1)}), bf16[8,64,128]{2,1,0:T(8,128)(2,1)S(1)}, u32[]{:S(2)}, u32[]{:S(2)}) %all-to-all-start.8) | async-done | bytes 131104 | tf_op jit(solution)/shard_map/all_to_all | solution.py:135
  (113 shorter events, 33.1 us)
Async XLA Ops:
  7.2 27.9 %copy-start.21 = (f32[512,1]{0,1:T(1,128)S(1)}, f32[512,1]{0,1:T(1,128)}, u32[]{:S(2)}) copy-start(f32[512,1]{0,1:T(1,128)} %param.25) | copy-start | bytes 6148
  7.2 27.9 %copy-start.16 = (bf16[512,128]{1,0:T(8,128)(2,1)S(1)}, bf16[512,128]{1,0:T(8,128)(2,1)}, u32[]{:S(2)}) copy-start(bf16[512,128]{1,0:T(8,128)(2,1)} %param.20) | copy-start | bytes 393220
  7.2 19.0 %copy-start.20 = (bf16[64,1024]{1,0:T(8,128)(2,1)S(1)}, bf16[64,1024]{1,0:T(8,128)(2,1)}, u32[]{:S(2)}) copy-start(bf16[64,1024]{1,0:T(8,128)(2,1)} %param.17) | copy-start | bytes 393220
  7.2 14.8 %all-to-all-start.1 = ((f32[64,8,1]{0,2,1:T(1,128)}), f32[64,8,1]{0,2,1:T(1,128)S(1)}, u32[]{:S(2)}, u32[]{:S(2)}) async-start(f32[64,8,1]{0,2,1:T(1,128)} %bitcast.168), calls=%async_computation.1 | async-start | bytes 8192 | tf_op jit(solution)/shard_map/all_to_all | solution.py:62
  15.7 28.2 %copy-start.11 = (bf16[512,128]{1,0:T(8,128)(2,1)S(1)}, bf16[512,128]{1,0:T(8,128)(2,1)}, u32[]{:S(2)}) copy-start(bf16[512,128]{1,0:T(8,128)(2,1)} %param.24) | copy-start | bytes 393220
  22.0 9.7 %all-to-all-start.4 = ((bf16[64,8,128]{2,0,1:T(8,128)(2,1)}), bf16[64,8,128]{2,0,1:T(8,128)(2,1)S(1)}, u32[]{:S(2)}, u32[]{:S(2)}) async-start(bf16[64,8,128]{2,0,1:T(8,128)(2,1)} %copy_bitcast_fusion.4), calls=%async_computation.4 | async-start | bytes 262144 | tf_op jit(solution)/shard_map/all_to_all | solution.py:57
  31.7 8.8 %all-to-all-start.5 = ((bf16[64,8,128]{2,0,1:T(8,128)(2,1)}), bf16[64,8,128]{2,0,1:T(8,128)(2,1)S(1)}, u32[]{:S(2)}, u32[]{:S(2)}) async-start(bf16[64,8,128]{2,0,1:T(8,128)(2,1)} %copy_bitcast_fusion.3), calls=%async_computation.5 | async-start | bytes 262144 | tf_op jit(solution)/shard_map/all_to_all | solution.py:58
  35.4 22.7 %copy-start.4 = (f32[512,512]{1,0:T(8,128)}, f32[512,512]{1,0:T(8,128)S(1)}, u32[]{:S(2)}) copy-start(f32[512,512]{1,0:T(8,128)S(1)} %fusion.23) | copy-start | bytes 3145732
  40.5 8.8 %all-to-all-start.2 = ((bf16[64,8,128]{2,0,1:T(8,128)(2,1)}), bf16[64,8,128]{2,0,1:T(8,128)(2,1)S(1)}, u32[]{:S(2)}, u32[]{:S(2)}) async-start(bf16[64,8,128]{2,0,1:T(8,128)(2,1)} %copy_bitcast_fusion.6), calls=%async_computation.2 | async-start | bytes 262144 | tf_op jit(solution)/shard_map/all_to_all | solution.py:59
  45.0 22.3 %copy-start.18 = (bf16[512,128]{1,0:T(8,128)(2,1)S(1)}, bf16[512,128]{1,0:T(8,128)(2,1)}, u32[]{:S(2)}) copy-start(bf16[512,128]{1,0:T(8,128)(2,1)} %param.22) | copy-start | bytes 393220
  49.3 8.8 %all-to-all-start.3 = ((bf16[64,8,128]{2,0,1:T(8,128)(2,1)}), bf16[64,8,128]{2,0,1:T(8,128)(2,1)S(1)}, u32[]{:S(2)}, u32[]{:S(2)}) async-start(bf16[64,8,128]{2,0,1:T(8,128)(2,1)} %copy_bitcast_fusion.5), calls=%async_computation.3 | async-start | bytes 262144 | tf_op jit(solution)/shard_map/all_to_all | solution.py:60
  58.1 8.8 %all-to-all-start = ((bf16[64,8,128]{2,0,1:T(8,128)(2,1)}), bf16[64,8,128]{2,0,1:T(8,128)(2,1)S(1)}, u32[]{:S(2)}, u32[]{:S(2)}) async-start(bf16[64,8,128]{2,0,1:T(8,128)(2,1)} %copy_bitcast_fusion.7), calls=%async_computation | async-start | bytes 262144 | tf_op jit(solution)/shard_map/all_to_all | solution.py:56
  61.5 69.4 %reduce-scatter.10.cloned.1.call-start = ((), (), s32[]{:S(2)}) async-start(), calls=%async_computation.16 | async-start | bytes 327680 | tf_op jit(solution)/shard_map/reduce_scatter | solution.py:138
  62.3 70.2 %reduce-scatter.12.cloned.1.call-start = ((), (), s32[]{:S(2)}) async-start(), calls=%async_computation.17 | async-start | bytes 327680 | tf_op jit(solution)/shard_map/reduce_scatter | solution.py:139
  67.6 38.7 %copy-start.9 = (bf16[512,512]{1,0:T(8,128)(2,1)}, bf16[512,512]{1,0:T(8,128)(2,1)S(1)}, u32[]{:S(2)}) copy-start(bf16[512,512]{1,0:T(8,128)(2,1)S(1)} %fusion.26) | copy-start | bytes 1572868
  88.8 45.0 %reduce-scatter.14.cloned.1.call-start = ((), (), s32[]{:S(2)}) async-start(), calls=%async_computation.18 | async-start | bytes 327680 | tf_op jit(solution)/shard_map/reduce_scatter | solution.py:142
  107.3 50.0 %reduce-scatter.6.cloned.1.call-start = ((), (), s32[]{:S(2)}) async-start(), calls=%async_computation.14 | async-start | bytes 1310720 | tf_op jit(solution)/shard_map/reduce_scatter | solution.py:124
  121.0 36.4 %copy-start.8 = (bf16[512,512]{1,0:T(8,128)(2,1)S(1)}, bf16[512,512]{1,0:T(8,128)(2,1)}, u32[]{:S(2)}) copy-start(bf16[512,512]{1,0:T(8,128)(2,1)} %copy-done.7) | copy-start | bytes 1572868
  121.0 36.4 %copy-start.17 = (bf16[512,128]{1,0:T(8,128)(2,1)S(1)}, bf16[512,128]{1,0:T(8,128)(2,1)}, u32[]{:S(2)}) copy-start(bf16[512,128]{1,0:T(8,128)(2,1)} %param.20) | copy-start | bytes 393220
  121.0 64.3 %reduce-scatter.8.cloned.1.call-start = ((), (), s32[]{:S(2)}) async-start(), calls=%async_computation.15 | async-start | bytes 1310720 | tf_op jit(solution)/shard_map/reduce_scatter | solution.py:125
  121.1 64.2 %copy-start.5 = (f32[512,512]{1,0:T(8,128)S(1)}, f32[512,512]{1,0:T(8,128)}, u32[]{:S(2)}) copy-start(f32[512,512]{1,0:T(8,128)} %copy-done.4) | copy-start | bytes 3145732
  121.1 64.2 %copy-start.12 = (bf16[512,128]{1,0:T(8,128)(2,1)S(1)}, bf16[512,128]{1,0:T(8,128)(2,1)}, u32[]{:S(2)}) copy-start(bf16[512,128]{1,0:T(8,128)(2,1)} %param.24) | copy-start | bytes 393220
  159.3 27.9 %all-to-all-start.7 = ((bf16[8,64,128]{2,1,0:T(8,128)(2,1)}), bf16[8,64,128]{2,1,0:T(8,128)(2,1)S(1)}, u32[]{:S(2)}, u32[]{:S(2)}) async-start(bf16[8,64,128]{2,1,0:T(8,128)(2,1)} %bitcast.21), calls=%async_computation.8 | async-start | bytes 262144 | tf_op jit(solution)/shard_map/all_to_all | solution.py:134
  187.2 9.1 %all-to-all-start.8 = ((bf16[8,64,128]{2,1,0:T(8,128)(2,1)}), bf16[8,64,128]{2,1,0:T(8,128)(2,1)S(1)}, u32[]{:S(2)}, u32[]{:S(2)}) async-start(bf16[8,64,128]{2,1,0:T(8,128)(2,1)} %bitcast.24), calls=%async_computation.10 | async-start | bytes 262144 | tf_op jit(solution)/shard_map/all_to_all | solution.py:135
  (16 other events, 54.0 us)
Sparse Core Ops, SparseCore 0:
  64.6 23.0 reduce-scatter.9
  89.9 19.1 reduce-scatter.11
  111.4 18.1 reduce-scatter.13
  131.8 25.5 reduce-scatter.5
  159.5 25.7 reduce-scatter.7
where the time goes:
time: 205 us; the launch traced here: 204 us
  waiting for transfers between devices  73.8 us (36%)
  blocking collectives  44.9 us (22%)
  starting transfers between devices  30.5 us (15%)
  matrix products  20.5 us (10%)
  local copies, waits for them, and re-layouts  14.2 us (7%)
  between operations  14.1 us (7%)
  other arithmetic  5.63 us (3%)
    reduce_scatter x1, waiting for transfers between devices, shards(): lax.psum_scatter(value_terms, 'inner', scatter_dimension=0, tiled=True)  22.3 us
    reduce_scatter x1, waiting for transfers between devices, shards(): lax.psum_scatter(key_terms, 'inner', scatter_dimension=0, tiled=True)  22 us
    all_gather x1, blocking collectives, shards(): lax.all_gather(keys, 'inner', axis=0, tiled=True)  19.9 us
    all_gather x1, blocking collectives, shards(): lax.all_gather(values, 'inner', axis=0, tiled=True)  17.1 us
    dot_general x10, matrix products, down_rows(): lax.dot_general(left, right, (((0,), (0,)), ((), ())), preferred_element_...  9.88 us
    all_to_all x1, blocking collectives, shards(): lax.all_to_all(head_grads[0], 'outer', split_axis=0, concat_axis=1, tiled...  7.89 us
    all_to_all x1, starting transfers between devices, shards(): lax.all_to_all(logsum_image, 'outer', split_axis=1, concat_axis=0, tiled=...  5.34 us
    dot_general x10, matrix products, across_rows(): lax.dot_general(left, right, (((1,), (1,)), ((), ())), preferred_element_...  5.31 us
  transfers between devices with their start and end apart: 13, of which 8 were waited for; matrix products, arithmetic and copies ran while one was open for 17% of the time, Pallas kernels for 0%

commit v1 on v0

v1 whole, which is shorter than its diff:
```python
import functools
import math

import jax
import jax.numpy as jnp
from jax import lax
from jax.experimental import pallas as pl
from jax.experimental.pallas import tpu as pltpu
from jax.sharding import PartitionSpec as P

HEAD_DIM = 128
LANES = 128
SNAKE = True
MESH = pl.DeviceIdType.MESH


def across_rows(left, right, **options):
    return lax.dot_general(
        left, right, (((1,), (1,)), ((), ())), preferred_element_type=jnp.float32, **options
    )


def kernel(
    dims,
    q_ref, k_ref, v_ref, o_ref, g_ref, l_ref,
    qt_ref, kt_ref, vt_ref, ot_ref, gt_ref, lt_ref,
    out_q, out_k, out_v, out_qt, out_kt, out_vt,
    qg, kv, key_flip, stat_send, stat, row_stat, own_o, own_g, text_o,
    dq_acc, dkv_acc, dq_send, dq_recv, dkv_send, dkv_recv, final,
    local_sem, text_sem, in_send, in_recv, gather_send, gather_recv,
    sum_send, sum_recv, out_send, out_recv,
):
    n_out, n_in, rows, columns, tokens, block, share = dims
    d = HEAD_DIM
    scale = HEAD_DIM ** (-0.5)
    o = lax.axis_index("outer")
    i = lax.axis_index("inner")

    def column_in(row, place):
        if not SNAKE:
            return place
        return place + (row % 2) * (columns - 1 - 2 * place)

    row = i // columns
    column = column_in(row, i % columns)

    def inner_of(row, column):
        return row * columns + column_in(row, column)

    def row_peer(a):
        return inner_of(row, (column + a) % columns)

    def column_peer(b):
        return inner_of((row + b) % rows, column)

    def other(k):
        return (o + k) % n_out

    own_loads = [
        pltpu.make_async_copy(g_ref, own_g, local_sem.at[0]),
        pltpu.make_async_copy(o_ref, own_o, local_sem.at[1]),
    ]
    for copy in own_loads:
        copy.start()

    barrier = pltpu.get_barrier_semaphore()
    for k in range(1, n_out):
        pl.semaphore_signal(barrier, inc=1, device_id=(other(k), i), device_id_type=MESH)
    for a in range(1, columns):
        pl.semaphore_signal(barrier, inc=1, device_id=(o, row_peer(a)), device_id_type=MESH)
    for b in range(1, rows):
        pl.semaphore_signal(barrier, inc=1, device_id=(o, column_peer(b)), device_id_type=MESH)

    text_loads = []

    def text_load(source, peer, target):
        copy = pltpu.make_async_copy(
            source.at[pl.ds(pl.multiple_of(peer * share, share), share)],
            target,
            text_sem.at[len(text_loads)],
        )
        copy.start()
        text_loads.append(copy)

    text = pl.ds(block, share)
    for b in range(rows):
        text_load(kt_ref, column_peer(b), kv.at[b, 0, text])
        text_load(vt_ref, column_peer(b), kv.at[b, 1, text])
    for a in range(columns):
        text_load(qt_ref, row_peer(a), qg.at[a, 0, text])
        text_load(gt_ref, row_peer(a), qg.at[a, 1, text])
        text_load(ot_ref, row_peer(a), text_o.at[a])

    pl.semaphore_wait(barrier, n_out - 1 + columns - 1 + rows - 1)

    own_rows = pl.ds(pl.multiple_of(o * tokens, tokens), tokens)

    def exchange(which, source, target, k):
        if k == 0:
            return pltpu.make_async_copy(source, target, in_recv.at[which, 0])
        return pltpu.make_async_remote_copy(
            src_ref=source,
            dst_ref=target,
            send_sem=in_send.at[which, k],
            recv_sem=in_recv.at[which, k],
            device_id=(other(k), i),
            device_id_type=MESH,
        )

    def head_of(ref, k):
        return ref.at[:, pl.ds(pl.multiple_of(other(k) * d, d), d)]

    homes = (kv.at[0, 0, own_rows], kv.at[0, 1, own_rows], qg.at[0, 0, own_rows], qg.at[0, 1, own_rows])
    arrivals = []
    for pair in ((0, 1), (2, 3)):
        for k in range(n_out):
            for which in pair:
                source = (k_ref, v_ref, q_ref, g_ref)[which]
                copy = exchange(which, head_of(source, k), homes[which], k)
                copy.start()
                arrivals.append((which, k, copy))

    for copy in own_loads:
        copy.wait()
    lane = lax.broadcasted_iota(jnp.int32, (1, LANES), 1)
    ones = jnp.ones((8, d), jnp.float32)
    repeats = LANES // tokens
    for h in range(n_out):
        cut = slice(h * d, (h + 1) * d)
        product = own_g[:, cut].astype(jnp.float32) * own_o[:, cut].astype(jnp.float32)
        product = jnp.concatenate([product] * repeats, axis=0)
        delta = across_rows(ones, product, precision=lax.Precision.HIGHEST)
        stat_send[h, 0:1, :] = l_ref[h : h + 1, :]
        stat_send[h, 1:2, :] = delta[0:1, :]
    for k in range(n_out):
        copy = exchange(4, stat_send.at[other(k)], stat.at[0, o], k)
        copy.start()
        arrivals.append((4, k, copy))

    for copy in text_loads:
        copy.wait()
    for a in range(columns):
        product = qg[a, 1, text].astype(jnp.float32) * text_o[a].astype(jnp.float32)
        delta = across_rows(ones, product, precision=lax.Precision.HIGHEST)
        row_stat[a, 0:1, text] = lt_ref[row_peer(a)]
        row_stat[a, 1:2, text] = delta[0:1, :]

    dq_acc[...] = jnp.zeros_like(dq_acc)
    dkv_acc[...] = jnp.zeros_like(dkv_acc)

    def gather(which, offset):
        group = rows if which < 2 else columns
        place = (group - offset) % group
        if which < 4:
            buffer = (kv, kv, qg, qg)[which]
            source = buffer.at[0, which % 2, pl.ds(0, block)]
            target = buffer.at[place, which % 2, pl.ds(0, block)]
        else:
            source, target = stat.at[0], stat.at[place]
        peer = column_peer(offset) if which < 2 else row_peer(offset)
        return pltpu.make_async_remote_copy(
            src_ref=source,
            dst_ref=target,
            send_sem=gather_send.at[which, offset],
            recv_sem=gather_recv.at[which, place],
            device_id=(o, peer),
            device_id_type=MESH,
        )

    for which in (0, 1, 2, 3, 4):
        for kind, k, copy in arrivals:
            if kind == which:
                if k == 0:
                    copy.wait()
                else:
                    copy.wait_recv()
        for offset in range(1, rows if which < 2 else columns):
            gather(which, offset).start()

    def spread_statistics(a):
        for start in range(0, block, LANES):
            first = start // tokens
            lines = [stat[a, first + p] for p in range(min(repeats, n_out - first))]
            merged = lines[0]
            for p in range(1, len(lines)):
                merged = jnp.where(lane // tokens == p, lines[p], merged)
            row_stat[a, :, start : start + LANES] = merged

    def flip_keys(b):
        key_flip[b] = kv[b, 0].astype(jnp.float32).T.astype(jnp.bfloat16)

    size = math.gcd(block, 256)
    chunks = [(start, size) for start in range(0, block, size)] + [(block, share)]

    def total(kind, offset):
        group = rows if kind else columns
        place = (group - offset) % group
        send, recv = ((dq_send, dq_recv), (dkv_send, dkv_recv))[kind]
        peer = column_peer(offset) if kind else row_peer(offset)
        return pltpu.make_async_remote_copy(
            src_ref=send.at[offset],
            dst_ref=recv.at[place],
            send_sem=sum_send.at[kind, offset],
            recv_sem=sum_recv.at[kind, place],
            device_id=(o, peer),
            device_id_type=MESH,
        )

    def query_sum(a):
        return dq_acc[a].T * scale

    def step(s, carry):
        a = s // rows
        turn = s % rows
        b = jnp.where(a == 0, turn, (turn + 1) % rows)

        @pl.when(a == 0)
        def _():
            @pl.when(b > 0)
            def _():
                gather(0, (rows - b) % rows).wait_recv()
                gather(1, (rows - b) % rows).wait_recv()

            flip_keys(b)

        @pl.when(turn == 0)
        def _():
            @pl.when(a > 0)
            def _():
                for which in (2, 3, 4):
                    gather(which, (columns - a) % columns).wait_recv()

            spread_statistics(a)

        keys, values, flipped = kv[b, 0], kv[b, 1], key_flip[b]
        for start, length in chunks:
            cut = slice(start, start + length)
            queries, upstream = qg[a, 0, cut], qg[a, 1, cut]
            scores = across_rows(keys, queries) * scale
            weights = jnp.exp(scores - row_stat[a, 0:1, cut])
            slopes = across_rows(values, upstream)
            mixed = (weights * (slopes - row_stat[a, 1:2, cut])).astype(jnp.bfloat16)
            weights = weights.astype(jnp.bfloat16)
            dkv_acc[b, 1] += jnp.dot(weights, upstream, preferred_element_type=jnp.float32)
            dkv_acc[b, 0] += jnp.dot(mixed, queries, preferred_element_type=jnp.float32)
            dq_acc[a, :, cut] += jnp.dot(flipped, mixed, preferred_element_type=jnp.float32)

        @pl.when(jnp.logical_and(a == columns - 1, b > 0))
        def _():
            dkv_send[b, 0] = (dkv_acc[b, 0] * scale).astype(jnp.bfloat16)
            dkv_send[b, 1] = dkv_acc[b, 1].astype(jnp.bfloat16)
            total(1, b).start()

        @pl.when(jnp.logical_and(a > 0, turn == rows - 1))
        def _():
            dq_send[a] = query_sum(a).astype(jnp.bfloat16)
            total(0, a).start()

        return carry

    lax.fori_loop(0, rows * columns, step, 0)

    outs = []

    def give_back(which, target):
        mine = pl.ds(pl.multiple_of(o * d, d), d)
        for k in range(n_out):
            piece = final.at[which, pl.ds(pl.multiple_of(other(k) * tokens, tokens), tokens)]
            if k == 0:
                copy = pltpu.make_async_copy(piece, target.at[:, mine], out_recv.at[which, 0])
            else:
                copy = pltpu.make_async_remote_copy(
                    src_ref=piece,
                    dst_ref=target.at[:, mine],
                    send_sem=out_send.at[which, k],
                    recv_sem=out_recv.at[which, k],
                    device_id=(other(k), i),
                    device_id_type=MESH,
                )
            copy.start()
            outs.append((k, copy))

    grad = query_sum(0)
    for a in range(1, columns):
        total(0, (columns - a) % columns).wait_recv()
        grad = grad + dq_recv[a].astype(jnp.float32)
    grad = grad.astype(jnp.bfloat16)
    final[0] = grad
    give_back(0, out_q)
    out_qt[...] = grad[block:]

    for b in range(1, rows):
        total(1, (rows - b) % rows).wait_recv()
    for part, image, own_text in ((0, out_k, out_kt), (1, out_v, out_vt)):
        grad = dkv_acc[0, part]
        if part == 0:
            grad = grad * scale
        for b in range(1, rows):
            grad = grad + dkv_recv[b, part].astype(jnp.float32)
        grad = grad.astype(jnp.bfloat16)
        final[1 + part] = grad
        give_back(1 + part, image)
        own_text[...] = grad[block:]

    for kind, k, copy in arrivals:
        if k > 0:
            copy.wait_send()
    for which in range(5):
        for offset in range(1, rows if which < 2 else columns):
            gather(which, offset).wait_send()
    for a in range(1, columns):
        total(0, a).wait_send()
    for b in range(1, rows):
        total(1, b).wait_send()
    for k, copy in outs:
        copy.wait()


def shards(
    mesh,
    query_image,
    key_image,
    value_image,
    attended_image,
    upstream_image,
    logsum_image,
    query_text,
    key_text,
    value_text,
    attended_text,
    upstream_text,
    logsum_text,
):
    n_out, n_in = mesh.shape["outer"], mesh.shape["inner"]
    columns = max(c for c in range(1, math.isqrt(n_in) + 1) if n_in % c == 0)
    rows = n_in // columns
    tokens, width = query_image.shape
    block = tokens * n_out
    share = query_text.shape[0] // n_in
    span = block + share
    d = HEAD_DIM
    image_lines = jnp.concatenate([logsum_image.T] * (LANES // tokens), axis=1)
    text_lines = logsum_text.reshape(n_in, 1, share)
    half, full = jnp.bfloat16, jnp.float32
    dma = pltpu.SemaphoreType.DMA
    vmem = pl.BlockSpec(memory_space=pltpu.VMEM)
    hbm = pl.BlockSpec(memory_space=pl.ANY)
    image_out = jax.ShapeDtypeStruct((tokens, width), half)
    text_out = jax.ShapeDtypeStruct((share, d), half)
    return pl.pallas_call(
        functools.partial(kernel, (n_out, n_in, rows, columns, tokens, block, share)),
        out_shape=(image_out,) * 3 + (text_out,) * 3,
        in_specs=[hbm] * 5 + [vmem] + [hbm] * 5 + [vmem],
        out_specs=(vmem,) * 6,
        scratch_shapes=[
            pltpu.VMEM((columns, 2, span, d), half),
            pltpu.VMEM((rows, 2, span, d), half),
            pltpu.VMEM((rows, d, span), half),
            pltpu.VMEM((n_out, 2, LANES), full),
            pltpu.VMEM((columns, n_out, 2, LANES), full),
            pltpu.VMEM((columns, 2, span), full),
            pltpu.VMEM((tokens, width), half),
            pltpu.VMEM((tokens, width), half),
            pltpu.VMEM((columns, share, d), half),
            pltpu.VMEM((columns, d, span), full),
            pltpu.VMEM((rows, 2, span, d), full),
            pltpu.VMEM((columns, span, d), half),
            pltpu.VMEM((columns, span, d), half),
            pltpu.VMEM((rows, 2, span, d), half),
            pltpu.VMEM((rows, 2, span, d), half),
            pltpu.VMEM((3, span, d), half),
            dma((2,)),
            dma((2 * rows + 3 * columns,)),
            dma((5, n_out)),
            dma((5, n_out)),
            dma((5, max(rows, columns))),
            dma((5, max(rows, columns))),
            dma((2, max(rows, columns))),
            dma((2, max(rows, columns))),
            dma((3, n_out)),
            dma((3, n_out)),
        ],
        compiler_params=pltpu.CompilerParams(collective_id=0, has_side_effects=True),
    )(
        query_image, key_image, value_image, attended_image, upstream_image, image_lines,
        query_text, key_text, value_text, attended_text, upstream_text, text_lines,
    )


def solution(mesh):
    tokens_spec = P(("outer", "inner"), None)
    return jax.shard_map(
        functools.partial(shards, mesh),
        mesh=mesh,
        in_specs=(tokens_spec,) * 6 + (P(None, "outer"),) * 6,
        out_specs=(tokens_spec,) * 3 + (P("inner", "outer"),) * 3,
        check_vma=False,
    )
```

time: 205 us -> 57 us (0.28)
  waiting for transfers between devices: 73.8 us -> 0 us
  Pallas kernels: 0 us -> 49 us
  blocking collectives: 44.9 us -> 0 us
  starting transfers between devices: 30.5 us -> 0 us
  matrix products: 20.5 us -> 0 us
  between operations: 14.1 us -> 0.66 us
  local copies, waits for them, and re-layouts: 14.2 us -> 5.47 us
  other arithmetic: 5.63 us -> 1.43 us
    pallas_call x0 -> x1, Pallas kernels: none -> 49 us  [shards(): pl.pallas_call(functools.partial(kernel, (n_out, n_in, rows, columns, tok...]
    reduce_scatter x5 -> x0, waiting for transfers between devices: 44.3 us -> none  [the longest x1 22.3 us: shards(): lax.psum_scatter(value_terms, 'inner', scatter_dimension=0, tiled=True)]
    all_gather x2 -> x0, blocking collectives: 37 us -> none  [the longest x1 19.9 us: shards(): lax.all_gather(keys, 'inner', axis=0, tiled=True)]
    all_to_all x8 -> x0, starting transfers between devices: 30.3 us -> none  [the longest x1 5.34 us: shards(): lax.all_to_all(logsum_image, 'outer', split_axis=1, concat_axis=0, tiled=...]
    all_to_all x8 -> x0, waiting for transfers between devices: 28.4 us -> none  [the longest x1 5.24 us: shards(): lax.all_to_all(attended_image, 'outer', split_axis=1, concat_axis=0, tile...]
    dot_general x25 -> x0, matrix products: 20.5 us -> none  [the longest x10 9.88 us: down_rows(): lax.dot_general(left, right, (((0,), (0,)), ((), ())), preferred_element_...]
    all_to_all x10 -> x0, local copies, waits for them, and re-layouts: 8.26 us -> none  [the longest x1 1.62 us: shards(): lax.all_to_all(value_image, 'outer', split_axis=1, concat_axis=0, tiled=T...]
    all_to_all x1 -> x0, blocking collectives: 7.89 us -> none  [shards(): lax.all_to_all(head_grads[0], 'outer', split_axis=0, concat_axis=1, tiled...]
  transfers between devices with their start and end apart: 13 -> 0, of which waited for: 8 -> 0; matrix products, arithmetic and copies ran while one was open for 17% -> 0% of each run, Pallas kernels for 0% -> 0%
where the time goes in v1:
time: 57 us; the launch traced here: 56.5 us
  Pallas kernels  49 us (86%)
  local copies, waits for them, and re-layouts  5.47 us (10%)
  other arithmetic  1.43 us (3%)
  between operations  0.66 us (1%)
    pallas_call x1, Pallas kernels, shards(): pl.pallas_call(functools.partial(kernel, (n_out, n_in, rows, columns, tok...  49 us
    unnamed x16, local copies, waits for them, and re-layouts  5.47 us
    concatenate x1, other arithmetic, shards(): image_lines = jnp.concatenate([logsum_image.T] * (LANES // tokens), axis=1)  1.43 us

profile of v1, /device:TPU:0, one launch (start us, length us, event | category | flops | bytes accessed | tf_op | source)
XLA Modules:
  0.0 56.5 jit_solution(5747230010073469514)
XLA Ops:
  0.6 1.4 %pad_maximum_fusion.l_ref = f32[8,128]{1,0:T(8,128)} fusion(f32[8,64]{1,0:T(8,128)} %bitcast.2), kind=kLoop, calls=%fused_computation | loop fusion | flops 1024 | bytes 6144 | tf_op jit(solution)/shard_map/concatenate | solution.py:342
  2.1 49.0 %shard_map.163 = (bf16[64,1024]{1,0:T(8,128)(2,1)}, bf16[64,1024]{1,0:T(8,128)(2,1)}, bf16[64,1024]{1,0:T(8,128)(2,1)}, bf16[128,128]{1,0:T(8,128)(2,1)}, bf16[1...) custom-call(bf16[64,1024]{1,0:T(8,128)(2,1)} %q_ref.1, bf16[64,1024]{1,0:T(8,128)(2,1)} %k_ref.1, bf16[64,1024]{1,0:T(8,128)(2,1)} %v_ref.1, ...), custom_call_target="tpu_custom_call" | custom-call | tf_op jit(solution)/shard_map/pallas_call | solution.py:350
  51.1 0.0 copy-start.1
  51.1 1.6 %copy.24 = bf16[64,1024]{1,0:T(8,128)(2,1)} copy(bf16[64,1024]{1,0:T(8,128)(2,1)} %get-tuple-element.12) | data formatting | bytes 262144
  52.7 0.0 copy-done.1
  52.7 0.0 copy-start
  52.7 0.7 %copy.25 = bf16[64,1024]{1,0:T(8,128)(2,1)} copy(bf16[64,1024]{1,0:T(8,128)(2,1)S(1)} %copy-done.1) | data formatting | bytes 262144
  53.3 0.3 copy-done
  53.6 0.0 copy-start.4
  53.6 0.7 %copy.26 = bf16[64,1024]{1,0:T(8,128)(2,1)} copy(bf16[64,1024]{1,0:T(8,128)(2,1)S(1)} %copy-done) | data formatting | bytes 262144
  54.3 0.1 copy-done.4
  54.4 0.0 copy-start.3
  54.4 0.6 %copy.27 = bf16[128,128]{1,0:T(8,128)(2,1)} copy(bf16[128,128]{1,0:T(8,128)(2,1)S(1)} %copy-done.4) | data formatting | bytes 65536
  55.0 0.2 copy-done.3
  55.2 0.0 copy-start.2
  55.2 0.6 %copy.28 = bf16[128,128]{1,0:T(8,128)(2,1)} copy(bf16[128,128]{1,0:T(8,128)(2,1)S(1)} %copy-done.3) | data formatting | bytes 65536
  55.8 0.2 copy-done.2
  55.9 0.6 %copy.29 = bf16[128,128]{1,0:T(8,128)(2,1)} copy(bf16[128,128]{1,0:T(8,128)(2,1)S(1)} %copy-done.2) | data formatting | bytes 65536
Async XLA Ops:
  51.1 1.6 %copy-start.1 = (bf16[64,1024]{1,0:T(8,128)(2,1)S(1)}, bf16[64,1024]{1,0:T(8,128)(2,1)}, u32[]{:S(2)}) copy-start(bf16[64,1024]{1,0:T(8,128)(2,1)} %get-tuple-element.13) | copy-start | bytes 393220
  52.7 1.0 %copy-start = (bf16[64,1024]{1,0:T(8,128)(2,1)S(1)}, bf16[64,1024]{1,0:T(8,128)(2,1)}, u32[]{:S(2)}) copy-start(bf16[64,1024]{1,0:T(8,128)(2,1)} %get-tuple-element.14) | copy-start | bytes 393220
  53.6 0.8 %copy-start.4 = (bf16[128,128]{1,0:T(8,128)(2,1)S(1)}, bf16[128,128]{1,0:T(8,128)(2,1)}, u32[]{:S(2)}) copy-start(bf16[128,128]{1,0:T(8,128)(2,1)} %get-tuple-element.15) | copy-start | bytes 98308
  54.4 0.8 %copy-start.3 = (bf16[128,128]{1,0:T(8,128)(2,1)S(1)}, bf16[128,128]{1,0:T(8,128)(2,1)}, u32[]{:S(2)}) copy-start(bf16[128,128]{1,0:T(8,128)(2,1)} %get-tuple-element.16) | copy-start | bytes 98308
  55.2 0.8 %copy-start.2 = (bf16[128,128]{1,0:T(8,128)(2,1)S(1)}, bf16[128,128]{1,0:T(8,128)(2,1)}, u32[]{:S(2)}) copy-start(bf16[128,128]{1,0:T(8,128)(2,1)} %get-tuple-element.17) | copy-start | bytes 98308

commit v2 on v1

v2 whole, which is shorter than its diff:
```python
import functools
import math

import jax
import jax.numpy as jnp
from jax import lax
from jax.experimental import pallas as pl
from jax.experimental.pallas import tpu as pltpu
from jax.sharding import PartitionSpec as P

HEAD_DIM = 128
LANES = 128
MESH = pl.DeviceIdType.MESH


def across_rows(left, right, **options):
    return lax.dot_general(
        left, right, (((1,), (1,)), ((), ())), preferred_element_type=jnp.float32, **options
    )


def kernel(
    dims,
    q_ref, k_ref, v_ref, o_ref, g_ref, l_ref,
    qt_ref, kt_ref, vt_ref, ot_ref, gt_ref, lt_ref,
    out_q, out_k, out_v, out_qt, out_kt, out_vt,
    qg, kv, key_flip, lines_in, stat_send, stat, row_stat, own_o, own_g, text_o,
    dq_acc, dkv_acc, dq_send, dq_recv, dkv_send, dkv_recv, final,
    local_sem, text_sem, in_send, in_recv, gather_send, gather_recv,
    sum_send, sum_recv, out_send, out_recv,
):
    n_out, n_in, rows, columns, tokens, block, share = dims
    span = block + share
    d = HEAD_DIM
    scale = HEAD_DIM ** (-0.5)
    o = lax.axis_index("outer")
    i = lax.axis_index("inner")

    line, place_in = i // rows, i % rows

    def row_peer(a):
        return (line + a) % columns * rows + place_in

    def column_peer(b):
        return line * rows + (place_in + b) % rows

    def other(k):
        return (o + k) % n_out

    own_loads = [
        pltpu.make_async_copy(g_ref, own_g, local_sem.at[0]),
        pltpu.make_async_copy(o_ref, own_o, local_sem.at[1]),
    ]
    for copy in own_loads:
        copy.start()

    barrier = pltpu.get_barrier_semaphore()
    for k in range(1, n_out):
        pl.semaphore_signal(barrier, inc=1, device_id=(other(k), i), device_id_type=MESH)
    for a in range(1, columns):
        pl.semaphore_signal(barrier, inc=1, device_id=(o, row_peer(a)), device_id_type=MESH)
    for b in range(1, rows):
        pl.semaphore_signal(barrier, inc=1, device_id=(o, column_peer(b)), device_id_type=MESH)

    text_loads = []

    def text_load(source, peer, target):
        copy = pltpu.make_async_copy(
            source.at[pl.ds(pl.multiple_of(peer * share, share), share)],
            target,
            text_sem.at[len(text_loads)],
        )
        copy.start()
        text_loads.append(copy)

    text = pl.ds(block, share)
    for b in range(rows):
        text_load(kt_ref, column_peer(b), kv.at[b, 0, text])
        text_load(vt_ref, column_peer(b), kv.at[b, 1, text])
    for a in range(columns):
        text_load(qt_ref, row_peer(a), qg.at[a, 0, text])
        text_load(gt_ref, row_peer(a), qg.at[a, 1, text])
        text_load(ot_ref, row_peer(a), text_o.at[a])

    pl.semaphore_wait(barrier, n_out - 1 + columns - 1 + rows - 1)

    def piece(k):
        return pl.ds(k * tokens, tokens)

    def exchange(which, source, target, k):
        if k == 0:
            return pltpu.make_async_copy(source, target, in_recv.at[which, 0])
        return pltpu.make_async_remote_copy(
            src_ref=source,
            dst_ref=target,
            send_sem=in_send.at[which, k],
            recv_sem=in_recv.at[which, k],
            device_id=(other(k), i),
            device_id_type=MESH,
        )

    def head_of(ref, k):
        return ref.at[:, pl.ds(pl.multiple_of(other(k) * d, d), d)]

    homes = (kv, kv, qg, qg)
    arrivals = {}
    for pair in ((2, 3), (0, 1)):
        for k in range(n_out):
            for which in pair:
                source = (k_ref, v_ref, q_ref, g_ref)[which]
                copy = exchange(which, head_of(source, k), homes[which].at[0, which % 2, piece(k)], k)
                copy.start()
                arrivals[which, k] = copy

    for copy in own_loads:
        copy.wait()
    lane = lax.broadcasted_iota(jnp.int32, (1, LANES), 1)
    ones = jnp.ones((8, d), jnp.float32)
    repeats = LANES // tokens
    lines_in[...] = jnp.zeros_like(lines_in)
    lines_in[:, 0:tokens] = l_ref[...]
    image_lines = lines_in[...]
    for p in range(1, repeats):
        moved = pltpu.roll(lines_in[...], p * tokens, 1)
        image_lines = jnp.where(lane // tokens == p, moved, image_lines)
    for h in range(n_out):
        cut = slice(h * d, (h + 1) * d)
        product = own_g[:, cut].astype(jnp.float32) * own_o[:, cut].astype(jnp.float32)
        product = jnp.concatenate([product] * repeats, axis=0)
        delta = across_rows(ones, product, precision=lax.Precision.HIGHEST)
        stat_send[h, 0:1, :] = image_lines[h : h + 1, :]
        stat_send[h, 1:2, :] = delta[0:1, :]
    for k in range(n_out):
        copy = exchange(4, stat_send.at[other(k)], stat.at[0, k], k)
        copy.start()
        arrivals[4, k] = copy

    for copy in text_loads:
        copy.wait()
    for a in range(columns):
        product = qg[a, 1, text].astype(jnp.float32) * text_o[a].astype(jnp.float32)
        delta = across_rows(ones, product, precision=lax.Precision.HIGHEST)
        row_stat[a, 0:1, text] = lt_ref[row_peer(a)]
        row_stat[a, 1:2, text] = delta[0:1, :]

    def gather(which, offset, k):
        group = rows if which < 2 else columns
        place = (group - offset) % group
        if which < 4:
            source = homes[which].at[0, which % 2, piece(k)]
            target = homes[which].at[place, which % 2, piece(k)]
        else:
            source, target = stat.at[0], stat.at[place]
        peer = column_peer(offset) if which < 2 else row_peer(offset)
        return pltpu.make_async_remote_copy(
            src_ref=source,
            dst_ref=target,
            send_sem=gather_send.at[which, offset, k],
            recv_sem=gather_recv.at[which, place, k],
            device_id=(o, peer),
            device_id_type=MESH,
        )

    def landed(which, k):
        if k == 0:
            arrivals[which, k].wait()
        else:
            arrivals[which, k].wait_recv()

    for k in range(n_out):
        for which in (2, 3):
            landed(which, k)
            for offset in range(1, columns):
                gather(which, offset, k).start()
    for k in range(n_out):
        landed(4, k)
    for offset in range(1, columns):
        gather(4, offset, 0).start()
    for k in range(n_out):
        for which in (0, 1):
            landed(which, k)
            for offset in range(1, rows):
                gather(which, offset, k).start()

    dq_acc[...] = jnp.zeros_like(dq_acc)
    dkv_acc[...] = jnp.zeros_like(dkv_acc)

    def spread_statistics(a):
        for start in range(0, block, LANES):
            first = start // tokens
            lines = [stat[a, first + p] for p in range(min(repeats, n_out - first))]
            merged = lines[0]
            for p in range(1, len(lines)):
                merged = jnp.where(lane // tokens == p, lines[p], merged)
            row_stat[a, :, start : start + LANES] = merged

    def flip_keys(b):
        key_flip[b] = kv[b, 0].astype(jnp.float32).T.astype(jnp.bfloat16)

    size = math.gcd(block, 256)
    chunks = [(start, size) for start in range(0, block, size)] + [(block, share)]
    halves = [(0, size), (size, span - size)]

    def total(kind, offset, n):
        group = rows if kind else columns
        place = (group - offset) % group
        start, length = (halves if kind else chunks)[n]
        cut = pl.ds(start, length)
        if kind:
            source, target = dkv_send.at[offset, kind - 1, cut], dkv_recv.at[place, kind - 1, cut]
        else:
            source, target = dq_send.at[offset, cut], dq_recv.at[place, cut]
        peer = column_peer(offset) if kind else row_peer(offset)
        return pltpu.make_async_remote_copy(
            src_ref=source,
            dst_ref=target,
            send_sem=sum_send.at[kind, offset, n],
            recv_sem=sum_recv.at[kind, place, n],
            device_id=(o, peer),
            device_id_type=MESH,
        )

    def query_sum(a, n):
        start, length = chunks[n]
        return dq_acc[a, :, start : start + length].T * scale

    def work(a, b, n):
        start, length = chunks[n]
        cut = slice(start, start + length)
        keys, values = kv[b, 0], kv[b, 1]
        queries, upstream = qg[a, 0, cut], qg[a, 1, cut]
        scores = across_rows(keys, queries) * scale
        weights = jnp.exp(scores - row_stat[a, 0:1, cut])
        slopes = across_rows(values, upstream)
        mixed = (weights * (slopes - row_stat[a, 1:2, cut])).astype(jnp.bfloat16)
        weights = weights.astype(jnp.bfloat16)
        dkv_acc[b, 1] += jnp.dot(weights, upstream, preferred_element_type=jnp.float32)
        dkv_acc[b, 0] += jnp.dot(mixed, queries, preferred_element_type=jnp.float32)
        dq_acc[a, :, cut] += jnp.dot(key_flip[b], mixed, preferred_element_type=jnp.float32)

    spread_statistics(0)
    flip_keys(0)
    for n in range(len(chunks)):
        work(0, 0, n)

    def near_keys(b, carry):
        for which in (0, 1):
            for k in range(n_out):
                gather(which, (rows - b) % rows, k).wait_recv()
        flip_keys(b)
        for n in range(len(chunks)):
            work(0, b, n)
        return carry

    lax.fori_loop(1, rows, near_keys, 0)

    def far_queries(a, carry):
        offset = (columns - a) % columns
        for n in (len(chunks) - 1, *range(len(chunks) - 1)):
            start, length = chunks[n]
            if start == 0:
                gather(4, offset, 0).wait_recv()
                spread_statistics(a)
            if start < block:
                for k in range(start // tokens, (start + length) // tokens):
                    gather(2, offset, k).wait_recv()
                    gather(3, offset, k).wait_recv()

            def with_keys(b, carry):
                work(a, b, n)
                return carry

            lax.fori_loop(0, rows, with_keys, 0)
            dq_send[a, start : start + length] = query_sum(a, n).astype(jnp.bfloat16)
            total(0, a, n).start()
        return carry

    lax.fori_loop(1, columns, far_queries, 0)

    for b in range(1, rows):
        for part in (0, 1):
            grad = dkv_acc[b, part]
            if part == 0:
                grad = grad * scale
            dkv_send[b, part] = grad.astype(jnp.bfloat16)
            for n in range(len(halves)):
                total(1 + part, b, n).start()

    outs = []
    mine = pl.ds(pl.multiple_of(o * d, d), d)

    def give_back(which, target, text_target, start, length):
        for k in range(start // tokens, min(start + length, block) // tokens):
            source = final.at[which, piece(k)]
            if k == 0:
                copy = pltpu.make_async_copy(source, target.at[:, mine], out_recv.at[which, 0])
            else:
                copy = pltpu.make_async_remote_copy(
                    src_ref=source,
                    dst_ref=target.at[:, mine],
                    send_sem=out_send.at[which, k],
                    recv_sem=out_recv.at[which, k],
                    device_id=((o + n_out - k) % n_out, i),
                    device_id_type=MESH,
                )
            copy.start()
            outs.append(copy)
        if start + length == span:
            copy = pltpu.make_async_copy(final.at[which, text], text_target, out_send.at[which, 0])
            copy.start()
            outs.append(copy)

    for n in (len(chunks) - 1, *range(len(chunks) - 1)):
        start, length = chunks[n]
        cut = slice(start, start + length)
        grad = query_sum(0, n)
        for a in range(1, columns):
            total(0, (columns - a) % columns, n).wait_recv()
            grad = grad + dq_recv[a, cut].astype(jnp.float32)
        final[0, cut] = grad.astype(jnp.bfloat16)
        give_back(0, out_q, out_qt, start, length)

    for part, image, own_text in ((0, out_k, out_kt), (1, out_v, out_vt)):
        for n, (start, length) in enumerate(halves):
            cut = slice(start, start + length)
            grad = dkv_acc[0, part, cut]
            if part == 0:
                grad = grad * scale
            for b in range(1, rows):
                total(1 + part, (rows - b) % rows, n).wait_recv()
                grad = grad + dkv_recv[b, part, cut].astype(jnp.float32)
            final[1 + part, cut] = grad.astype(jnp.bfloat16)
            give_back(1 + part, image, own_text, start, length)

    for (which, k), copy in arrivals.items():
        if k > 0:
            copy.wait_send()
    for which in range(4):
        for offset in range(1, rows if which < 2 else columns):
            for k in range(n_out):
                gather(which, offset, k).wait_send()
    for a in range(1, columns):
        gather(4, a, 0).wait_send()
        for n in range(len(chunks)):
            total(0, a, n).wait_send()
    for b in range(1, rows):
        for n in range(len(halves)):
            total(1, b, n).wait_send()
            total(2, b, n).wait_send()
    for copy in outs:
        copy.wait()


def tail(*refs):
    sources, targets, held = refs[:6], refs[6:12], refs[12:18]
    sem = refs[18]
    loads = [pltpu.make_async_copy(s, h, sem.at[0, n]) for n, (s, h) in enumerate(zip(sources, held))]
    stores = [pltpu.make_async_copy(h, t, sem.at[1, n]) for n, (h, t) in enumerate(zip(held, targets))]
    for load in loads:
        load.start()
    for load, store in zip(loads, stores):
        load.wait()
        store.start()
    for store in stores:
        store.wait()


def shards(
    mesh,
    query_image,
    key_image,
    value_image,
    attended_image,
    upstream_image,
    logsum_image,
    query_text,
    key_text,
    value_text,
    attended_text,
    upstream_text,
    logsum_text,
):
    n_out, n_in = mesh.shape["outer"], mesh.shape["inner"]
    rows = max(c for c in range(1, math.isqrt(n_in) + 1) if n_in % c == 0)
    columns = n_in // rows
    tokens, width = query_image.shape
    block = tokens * n_out
    share = query_text.shape[0] // n_in
    span = block + share
    d = HEAD_DIM
    text_lines = logsum_text.reshape(n_in, 1, share)
    half, full = jnp.bfloat16, jnp.float32
    dma = pltpu.SemaphoreType.DMA
    vmem = pl.BlockSpec(memory_space=pltpu.VMEM)
    hbm = pl.BlockSpec(memory_space=pl.ANY)
    image_out = jax.ShapeDtypeStruct((tokens, width), half)
    text_out = jax.ShapeDtypeStruct((share, d), half)
    grads = pl.pallas_call(
        functools.partial(kernel, (n_out, n_in, rows, columns, tokens, block, share)),
        out_shape=(image_out,) * 3 + (text_out,) * 3,
        in_specs=[hbm] * 5 + [vmem] + [hbm] * 5 + [vmem],
        out_specs=(hbm,) * 6,
        scratch_shapes=[
            pltpu.VMEM((columns, 2, span, d), half),
            pltpu.VMEM((rows, 2, span, d), half),
            pltpu.VMEM((rows, d, span), half),
            pltpu.VMEM((n_out, LANES), full),
            pltpu.VMEM((n_out, 2, LANES), full),
            pltpu.VMEM((columns, n_out, 2, LANES), full),
            pltpu.VMEM((columns, 2, span), full),
            pltpu.VMEM((tokens, width), half),
            pltpu.VMEM((tokens, width), half),
            pltpu.VMEM((columns, share, d), half),
            pltpu.VMEM((columns, d, span), full),
            pltpu.VMEM((rows, 2, span, d), full),
            pltpu.VMEM((columns, span, d), half),
            pltpu.VMEM((columns, span, d), half),
            pltpu.VMEM((rows, 2, span, d), half),
            pltpu.VMEM((rows, 2, span, d), half),
            pltpu.VMEM((3, span, d), half),
            dma((2,)),
            dma((2 * rows + 3 * columns,)),
            dma((5, n_out)),
            dma((5, n_out)),
            dma((5, max(rows, columns), n_out)),
            dma((5, max(rows, columns), n_out)),
            dma((3, max(rows, columns), 1 + block // math.gcd(block, 256))),
            dma((3, max(rows, columns), 1 + block // math.gcd(block, 256))),
            dma((3, n_out)),
            dma((3, n_out)),
        ],
        compiler_params=pltpu.CompilerParams(collective_id=0, has_side_effects=True),
    )(
        query_image, key_image, value_image, attended_image, upstream_image, logsum_image.T,
        query_text, key_text, value_text, attended_text, upstream_text, text_lines,
    )
    return pl.pallas_call(
        tail,
        out_shape=(image_out,) * 3 + (text_out,) * 3,
        in_specs=[hbm] * 6,
        out_specs=(hbm,) * 6,
        scratch_shapes=[pltpu.VMEM((tokens, width), half)] * 3
        + [pltpu.VMEM((share, d), half)] * 3
        + [dma((2, 6))],
    )(*grads)


def solution(mesh):
    tokens_spec = P(("outer", "inner"), None)
    return jax.shard_map(
        functools.partial(shards, mesh),
        mesh=mesh,
        in_specs=(tokens_spec,) * 6 + (P(None, "outer"),) * 6,
        out_specs=(tokens_spec,) * 3 + (P("inner", "outer"),) * 3,
        check_vma=False,
    )
```

time: 57 us -> 51.9 us (0.911)
  the two profiles are of different devices: /device:TPU:0 before, /device:TPU:16 now
where the time goes in v2:
time: 51.9 us; the launch traced here: 51.7 us
  Pallas kernels  51.1 us (98%)
  between operations  0.64 us (1%)
    pallas_call x1, Pallas kernels, shards(): pl.pallas_call(functools.partial(kernel, (n_out, n_in, rows, columns, tok...  49.2 us
    pallas_call x1, Pallas kernels, shards(): pl.pallas_call(tail, out_shape=(image_out,) * 3 + (text_out,) * 3, in_spe...  1.82 us

profile of v2, /device:TPU:16, one launch (start us, length us, event | category | flops | bytes accessed | tf_op | source)
XLA Modules:
  0.0 51.7 jit_solution(9754501088473909873)
XLA Ops:
  0.6 49.2 %shard_map.163 = (bf16[64,1024]{1,0:T(8,128)(2,1)}, bf16[64,1024]{1,0:T(8,128)(2,1)}, bf16[64,1024]{1,0:T(8,128)(2,1)}, bf16[128,128]{1,0:T(8,128)(2,1)}, bf16[1...) custom-call(bf16[64,1024]{1,0:T(8,128)(2,1)} %q_ref.1, bf16[64,1024]{1,0:T(8,128)(2,1)} %k_ref.1, bf16[64,1024]{1,0:T(8,128)(2,1)} %v_ref.1, ...), custom_call_target="tpu_custom_call" | custom-call | tf_op jit(solution)/shard_map/pallas_call | solution.py:398
  49.9 1.8 %shard_map.164 = (bf16[64,1024]{1,0:T(8,128)(2,1)}, bf16[64,1024]{1,0:T(8,128)(2,1)}, bf16[64,1024]{1,0:T(8,128)(2,1)}, bf16[128,128]{1,0:T(8,128)(2,1)}, bf16[1...) custom-call(bf16[64,1024]{1,0:T(8,128)(2,1)} %get-tuple-element.12.refs_0_, bf16[64,1024]{1,0:T(8,128)(2,1)} %get-tuple-element.13.refs_1_, ...), custom_call_target="tpu_custom_call" | custom-call | tf_op jit(solution)/shard_map/pallas_call | solution.py:437

commit v3 on v2

--- a/solution.py
+++ b/solution.py
@@ -103,14 +103,32 @@
         return ref.at[:, pl.ds(pl.multiple_of(other(k) * d, d), d)]
 
     homes = (kv, kv, qg, qg)
-    arrivals = {}
-    for pair in ((2, 3), (0, 1)):
+
+    def arrival(which, k):
+        if which == 4:
+            return exchange(4, stat_send.at[other(k)], stat.at[0, k], k)
+        source = (k_ref, v_ref, q_ref, g_ref)[which]
+        return exchange(which, head_of(source, k), homes[which].at[0, which % 2, piece(k)], k)
+
+    at_end = jnp.logical_or(i == 0, i == n_in - 1)
+
+    def ordered(first, second):
+        @pl.when(at_end)
+        def _():
+            first()
+            second()
+
+        @pl.when(jnp.logical_not(at_end))
+        def _():
+            second()
+            first()
+
+    def depart(pair):
         for k in range(n_out):
             for which in pair:
-                source = (k_ref, v_ref, q_ref, g_ref)[which]
-                copy = exchange(which, head_of(source, k), homes[which].at[0, which % 2, piece(k)], k)
-                copy.start()
-                arrivals[which, k] = copy
+                arrival(which, k).start()
+
+    ordered(lambda: depart((0, 1)), lambda: depart((2, 3)))
 
     for copy in own_loads:
         copy.wait()
@@ -131,9 +149,7 @@
         stat_send[h, 0:1, :] = image_lines[h : h + 1, :]
         stat_send[h, 1:2, :] = delta[0:1, :]
     for k in range(n_out):
-        copy = exchange(4, stat_send.at[other(k)], stat.at[0, k], k)
-        copy.start()
-        arrivals[4, k] = copy
+        arrival(4, k).start()
 
     for copy in text_loads:
         copy.wait()
@@ -163,24 +179,22 @@
 
     def landed(which, k):
         if k == 0:
-            arrivals[which, k].wait()
+            arrival(which, k).wait()
         else:
-            arrivals[which, k].wait_recv()
-
-    for k in range(n_out):
-        for which in (2, 3):
-            landed(which, k)
-            for offset in range(1, columns):
-                gather(which, offset, k).start()
+            arrival(which, k).wait_recv()
+
+    def forward(pair, group):
+        for k in range(n_out):
+            for which in pair:
+                landed(which, k)
+                for offset in range(1, group):
+                    gather(which, offset, k).start()
+
+    ordered(lambda: forward((0, 1), rows), lambda: forward((2, 3), columns))
     for k in range(n_out):
         landed(4, k)
     for offset in range(1, columns):
         gather(4, offset, 0).start()
-    for k in range(n_out):
-        for which in (0, 1):
-            landed(which, k)
-            for offset in range(1, rows):
-                gather(which, offset, k).start()
 
     dq_acc[...] = jnp.zeros_like(dq_acc)
     dkv_acc[...] = jnp.zeros_like(dkv_acc)
@@ -243,98 +257,142 @@
     for n in range(len(chunks)):
         work(0, 0, n)
 
-    def near_keys(b, carry):
+    def near_keys_landed(b):
         for which in (0, 1):
             for k in range(n_out):
                 gather(which, (rows - b) % rows, k).wait_recv()
         flip_keys(b)
-        for n in range(len(chunks)):
-            work(0, b, n)
-        return carry
-
-    lax.fori_loop(1, rows, near_keys, 0)
-
-    def far_queries(a, carry):
-        offset = (columns - a) % columns
-        for n in (len(chunks) - 1, *range(len(chunks) - 1)):
+
+    def far_queries_landed(a, n):
+        start, length = chunks[n]
+        if start < block:
+            for k in range(start // tokens, (start + length) // tokens):
+                gather(2, (columns - a) % columns, k).wait_recv()
+                gather(3, (columns - a) % columns, k).wait_recv()
+        if start == 0:
+            gather(4, (columns - a) % columns, 0).wait_recv()
+            spread_statistics(a)
+
+    def send_queries(a, n):
+        start, length = chunks[n]
+        dq_send[a, start : start + length] = query_sum(a, n).astype(jnp.bfloat16)
+        total(0, a, n).start()
+
+    def send_keys(b):
+        for part in (0, 1):
+            for n, (start, length) in enumerate(halves):
+                cut = slice(start, start + length)
+                grad = dkv_acc[b, part, cut]
+                if part == 0:
+                    grad = grad * scale
+                dkv_send[b, part, cut] = grad.astype(jnp.bfloat16)
+                total(1 + part, b, n).start()
+
+    places = (len(chunks) - 1, *range(len(chunks) - 1))
+
+    def loop(first, last, body):
+        def with_carry(index, carry):
+            body(index)
+            return carry
+
+        lax.fori_loop(first, last, with_carry, 0)
+
+    @pl.when(jnp.logical_not(at_end))
+    def _():
+        def near_keys(b):
+            near_keys_landed(b)
+            for n in places:
+                work(0, b, n)
+
+        def far_queries(a):
+            for n in places:
+                far_queries_landed(a, n)
+                loop(0, rows, lambda b: work(a, b, n))
+                send_queries(a, n)
+
+        loop(1, rows, near_keys)
+        loop(1, columns, far_queries)
+        loop(1, rows, send_keys)
+
+    @pl.when(at_end)
+    def _():
+        def far_queries(a):
+            for n in places:
+                far_queries_landed(a, n)
+                work(a, 0, n)
+
+        def near_keys(b):
+            near_keys_landed(b)
+
+            def with_queries(a):
+                for n in places:
+                    work(a, b, n)
+
+            loop(0, columns, with_queries)
+            send_keys(b)
+
+        def give_queries(a):
+            for n in places:
+                send_queries(a, n)
+
+        loop(1, columns, far_queries)
+        loop(1, rows, near_keys)
+        loop(1, columns, give_queries)
+
+    mine = pl.ds(pl.multiple_of(o * d, d), d)
+    images, texts = (out_q, out_k, out_v), (out_qt, out_kt, out_vt)
+
+    def out_copy(which, k):
+        source, target = final.at[which, piece(k)], images[which].at[:, mine]
+        if k == 0:
+            return pltpu.make_async_copy(source, target, out_recv.at[which, 0])
+        return pltpu.make_async_remote_copy(
+            src_ref=source,
+            dst_ref=target,
+            send_sem=out_send.at[which, k],
+            recv_sem=out_recv.at[which, k],
+            device_id=((o + n_out - k) % n_out, i),
+            device_id_type=MESH,
+        )
+
+    def text_copy(which):
+        return pltpu.make_async_copy(final.at[which, text], texts[which], out_send.at[which, 0])
+
+    def give_back(which, start, length):
+        for k in range(start // tokens, min(start + length, block) // tokens):
+            out_copy(which, k).start()
+        if start + length == span:
+            text_copy(which).start()
+
+    def finish_queries():
+        for n in places:
             start, length = chunks[n]
-            if start == 0:
-                gather(4, offset, 0).wait_recv()
-                spread_statistics(a)
-            if start < block:
-                for k in range(start // tokens, (start + length) // tokens):
-                    gather(2, offset, k).wait_recv()
-                    gather(3, offset, k).wait_recv()
-
-            def with_keys(b, carry):
-                work(a, b, n)
-                return carry
-
-            lax.fori_loop(0, rows, with_keys, 0)
-            dq_send[a, start : start + length] = query_sum(a, n).astype(jnp.bfloat16)
-            total(0, a, n).start()
-        return carry
-
-    lax.fori_loop(1, columns, far_queries, 0)
-
-    for b in range(1, rows):
+            cut = slice(start, start + length)
+            grad = query_sum(0, n)
+            for a in range(1, columns):
+                total(0, (columns - a) % columns, n).wait_recv()
+                grad = grad + dq_recv[a, cut].astype(jnp.float32)
+            final[0, cut] = grad.astype(jnp.bfloat16)
+            give_back(0, start, length)
+
+    def finish_keys():
         for part in (0, 1):
-            grad = dkv_acc[b, part]
-            if part == 0:
-                grad = grad * scale
-            dkv_send[b, part] = grad.astype(jnp.bfloat16)
-            for n in range(len(halves)):
-                total(1 + part, b, n).start()
-
-    outs = []
-    mine = pl.ds(pl.multiple_of(o * d, d), d)
-
-    def give_back(which, target, text_target, start, length):
-        for k in range(start // tokens, min(start + length, block) // tokens):
-            source = final.at[which, piece(k)]
-            if k == 0:
-                copy = pltpu.make_async_copy(source, target.at[:, mine], out_recv.at[which, 0])
-            else:
-                copy = pltpu.make_async_remote_copy(
-                    src_ref=source,
-                    dst_ref=target.at[:, mine],
-                    send_sem=out_send.at[which, k],
-                    recv_sem=out_recv.at[which, k],
-                    device_id=((o + n_out - k) % n_out, i),
-                    device_id_type=MESH,
-                )
-            copy.start()
-            outs.append(copy)
-        if start + length == span:
-            copy = pltpu.make_async_copy(final.at[which, text], text_target, out_send.at[which, 0])
-            copy.start()
-            outs.append(copy)
-
-    for n in (len(chunks) - 1, *range(len(chunks) - 1)):
-        start, length = chunks[n]
-        cut = slice(start, start + length)
-        grad = query_sum(0, n)
-        for a in range(1, columns):
-            total(0, (columns - a) % columns, n).wait_recv()
-            grad = grad + dq_recv[a, cut].astype(jnp.float32)
-        final[0, cut] = grad.astype(jnp.bfloat16)
-        give_back(0, out_q, out_qt, start, length)
-
-    for part, image, own_text in ((0, out_k, out_kt), (1, out_v, out_vt)):
-        for n, (start, length) in enumerate(halves):
-            cut = slice(start, start + length)
-            grad = dkv_acc[0, part, cut]
-            if part == 0:
-                grad = grad * scale
-            for b in range(1, rows):
-                total(1 + part, (rows - b) % rows, n).wait_recv()
-                grad = grad + dkv_recv[b, part, cut].astype(jnp.float32)
-            final[1 + part, cut] = grad.astype(jnp.bfloat16)
-            give_back(1 + part, image, own_text, start, length)
-
-    for (which, k), copy in arrivals.items():
-        if k > 0:
-            copy.wait_send()
+            for n, (start, length) in enumerate(halves):
+                cut = slice(start, start + length)
+                grad = dkv_acc[0, part, cut]
+                if part == 0:
+                    grad = grad * scale
+                for b in range(1, rows):
+                    total(1 + part, (rows - b) % rows, n).wait_recv()
+                    grad = grad + dkv_recv[b, part, cut].astype(jnp.float32)
+                final[1 + part, cut] = grad.astype(jnp.bfloat16)
+                give_back(1 + part, start, length)
+
+    ordered(finish_queries, finish_keys)
+
+    for which in range(5):
+        for k in range(1, n_out):
+            arrival(which, k).wait_send()
     for which in range(4):
         for offset in range(1, rows if which < 2 else columns):
             for k in range(n_out):
@@ -347,8 +405,10 @@
         for n in range(len(halves)):
             total(1, b, n).wait_send()
             total(2, b, n).wait_send()
-    for copy in outs:
-        copy.wait()
+    for which in range(3):
+        text_copy(which).wait()
+        for k in range(n_out):
+            out_copy(which, k).wait()
 
 
 def tail(*refs):

time: 51.9 us -> 45.8 us (0.88)
  the two profiles are of different devices: /device:TPU:16 before, /device:TPU:8 now
where the time goes in v3:
time: 45.8 us; the launch traced here: 45.6 us
  Pallas kernels  45 us (98%)
  between operations  0.64 us (1%)
    pallas_call x1, Pallas kernels, shards(): pl.pallas_call(functools.partial(kernel, (n_out, n_in, rows, columns, tok...  43.1 us
    pallas_call x1, Pallas kernels, shards(): pl.pallas_call(tail, out_shape=(image_out,) * 3 + (text_out,) * 3, in_spe...  1.82 us

profile of v3, /device:TPU:8, one launch (start us, length us, event | category | flops | bytes accessed | tf_op | source)
XLA Modules:
  0.0 45.6 jit_solution(13354403005360710037)
XLA Ops:
  0.6 43.1 %shard_map.163 = (bf16[64,1024]{1,0:T(8,128)(2,1)}, bf16[64,1024]{1,0:T(8,128)(2,1)}, bf16[64,1024]{1,0:T(8,128)(2,1)}, bf16[128,128]{1,0:T(8,128)(2,1)}, bf16[1...) custom-call(bf16[64,1024]{1,0:T(8,128)(2,1)} %q_ref.1, bf16[64,1024]{1,0:T(8,128)(2,1)} %k_ref.1, bf16[64,1024]{1,0:T(8,128)(2,1)} %v_ref.1, ...), custom_call_target="tpu_custom_call" | custom-call | tf_op jit(solution)/shard_map/pallas_call | solution.py:458
  43.8 1.8 %shard_map.164 = (bf16[64,1024]{1,0:T(8,128)(2,1)}, bf16[64,1024]{1,0:T(8,128)(2,1)}, bf16[64,1024]{1,0:T(8,128)(2,1)}, bf16[128,128]{1,0:T(8,128)(2,1)}, bf16[1...) custom-call(bf16[64,1024]{1,0:T(8,128)(2,1)} %get-tuple-element.12.refs_0_, bf16[64,1024]{1,0:T(8,128)(2,1)} %get-tuple-element.13.refs_1_, ...), custom_call_target="tpu_custom_call" | custom-call | tf_op jit(solution)/shard_map/pallas_call | solution.py:497
